TPU v7x, 256 devices: a whole 4x4x8 slice. The times are simulated.
256 devices in a mesh: dp: 32 (over z_lo, x, core), expert: 8 (over z_hi, y).
Axes of the slice: x: 4, y: 4, z: 8 (z_hi: 2, z_lo: 4; z = z_hi * 4 + z_lo), core: 2. Of those that a mesh axis runs over, the one named last changes fastest.
Arguments:
- acts: float32 [65536, 1024], P(('dp', 'expert')), may hold values from -18 to 18, as said below
- grads_out: float32 [65536, 1024], P(('dp', 'expert')), may hold values from -18 to 18, as said below
- routes: int32 [65536, 2], P(('dp', 'expert')), may hold values from 0 to 7, all different within a row; in each aligned block of 256 rows (0 to 255, 256 to 511, ...) at most 96 rows name the same one
- counts: int32 [256, 8], P(('dp', 'expert')), may hold values from 48 to 96
- old_act_factor: float32 [8, 1024, 1024], P('expert', 'dp'), may hold values from -1 to 4, as said below
- old_grad_factor: float32 [8, 1024, 1024], P('expert', 'dp'), may hold values from -1 to 4, as said below
- momentum: float32 [8, 1024, 1024], P('expert', 'dp'), may hold values from -0.0018 to 0.0018
- weights: float32 [8, 1024, 1024], P('expert', 'dp'), may hold values from -0.1875 to 0.1875
Outputs:
- act_factor: float32 [8, 1024, 1024], P('expert', 'dp')
- grad_factor: float32 [8, 1024, 1024], P('expert', 'dp')
- new_momentum: float32 [8, 1024, 1024], P('expert', 'dp')
- new_weights: float32 [8, 1024, 1024], P('expert', 'dp')
Inputs may be any that keep to these rules, and one draw needn't show every extreme that they name: `acts`: entries are independent across rows; each feature has its own scale. `grads_out`: entries are independent across rows; each feature has its own scale. `old_act_factor`: each expert's matrix is symmetric, and each diagonal entry exceeds the sum of the magnitudes of the other entries of its row. `old_grad_factor`: each expert's matrix is symmetric, and each diagonal entry exceeds the sum of the magnitudes of the other entries of its row. `routes`: within the rows of one device no expert is named by more than 96 rows.
All inputs are finite; a program needn't handle non-finite values. Where the computation divides by a largest or mean magnitude, that divisor is 1e-20 or more.
Results may differ from a plain program's by a relative error of at most 0.00013.
Values sent between devices are 32-bit elements; how exact they have to be, the bound alone decides.
A program may use at most 128 MiB of HBM per device.

v0:
```python
import jax
import jax.numpy as jnp
from jax import lax
from jax.sharding import PartitionSpec as P


def product(left, right):
    return jnp.dot(left, right, precision=lax.Precision.HIGHEST, preferred_element_type=jnp.float32)


def inner_rows(left, right):
    return jnp.einsum(
        "rc,rf->cf",
        left,
        right,
        precision=lax.Precision.HIGHEST,
        preferred_element_type=jnp.float32,
    )


def first_iterate(factor):
    size = factor.shape[0]
    unit = jnp.eye(size, dtype=jnp.float32)
    damp = 0.1 * jnp.trace(factor) / size
    shifted = factor + damp * unit
    alpha = 1.0 / jnp.max(jnp.sum(jnp.abs(shifted), axis=1))
    return (shifted, alpha * (2.0 * unit - alpha * shifted))


def on_device(acts, grads_out, routes, counts, old_act_factor, old_grad_factor, momentum, weights):
    n_expert = lax.axis_size("expert")
    exp_dev = weights.shape[0]
    n_all = n_expert * exp_dev
    samples = routes.shape[0]
    feat = acts.shape[1]
    block = weights.shape[1]
    capacity = min(samples, 3 * samples * routes.shape[1] // (2 * n_all))
    experts = jnp.arange(n_all, dtype=jnp.int32)
    hit = jnp.sum(
        (routes[:, :, None] == experts[None, None, :]).astype(jnp.int32), axis=1, dtype=jnp.int32
    )
    rank = jnp.cumsum(hit, axis=0, dtype=jnp.int32) - hit
    keep = hit * (rank < counts[0][None, :]).astype(jnp.int32)
    slot_ids = jnp.arange(capacity, dtype=jnp.int32)
    match = hit[:, :, None] * (rank[:, :, None] == slot_ids[None, None, :]).astype(jnp.int32)
    row_ids = jnp.arange(samples, dtype=jnp.int32)
    source = jnp.sum(match * row_ids[:, None, None], axis=0, dtype=jnp.int32)
    present = jnp.sum(match * keep[:, :, None], axis=0, dtype=jnp.int32).astype(jnp.float32)
    sent_acts = jnp.take(acts, source, axis=0) * present[:, :, None]
    sent_grads = jnp.take(grads_out, source, axis=0) * present[:, :, None]
    got_acts, got_grads, got_present = (
        lax.all_to_all(sent_acts, "expert", split_axis=0, concat_axis=1, tiled=True),
        lax.all_to_all(sent_grads, "expert", split_axis=0, concat_axis=1, tiled=True),
        lax.all_to_all(present, "expert", split_axis=0, concat_axis=1, tiled=True),
    )
    mine = lax.psum(jnp.sum(got_present, axis=1), "dp")
    total = jnp.maximum(mine, jnp.float32(1.0))
    pieces = []
    local = 0
    act_cols = got_acts[local]
    grad_cols = got_grads[local]
    pieces.append(inner_rows(act_cols, got_acts[local]))
    pieces.append(inner_rows(grad_cols, got_grads[local]))
    pieces.append(inner_rows(grad_cols, got_acts[local]))
    stats = lax.psum_scatter(jnp.concatenate(pieces, axis=1), "dp", scatter_dimension=0, tiled=True)
    act_new = jnp.stack([stats[:, 0:feat] / total[0]])
    grad_new = jnp.stack([stats[:, feat : 2 * feat] / total[0]])
    act_factor = 0.5 * old_act_factor + 0.5 * act_new
    grad_factor = 0.5 * old_grad_factor + 0.5 * grad_new
    gradient_rows = jnp.stack([stats[:, 2 * feat : 3 * feat] / total[0]])
    full_act, full_grad, gradient_full = (
        lax.all_gather(act_factor, "dp", axis=1, tiled=True),
        lax.all_gather(grad_factor, "dp", axis=1, tiled=True),
        lax.all_gather(gradient_rows, "dp", axis=1, tiled=True),
    )
    offset = lax.axis_index("dp") * block
    local = 0
    shifted_act, first_act = first_iterate(full_act[local])
    shifted_grad, first_grad = first_iterate(full_grad[local])
    first_rows = lax.dynamic_slice_in_dim(first_grad, offset, block, 0)
    inverse_rows = 2.0 * first_rows - product(product(first_rows, shifted_grad), first_grad)
    left_side = product(inverse_rows, gradient_full[local])
    half_way = product(left_side, first_act)
    precond = 2.0 * half_way - product(product(half_way, shifted_act), first_act)
    moment_new = 0.9 * momentum[local] + precond
    moments = [moment_new]
    updates = [weights[local] - 0.5 * moment_new]
    return (act_factor, grad_factor, jnp.stack(moments), jnp.stack(updates))


def solution(mesh):
    in_specs = (
        P(("dp", "expert"), None),
        P(("dp", "expert"), None),
        P(("dp", "expert"), None),
        P(("dp", "expert"), None),
        P("expert", "dp", None),
        P("expert", "dp", None),
        P("expert", "dp", None),
        P("expert", "dp", None),
    )
    out_specs = (
        P("expert", "dp", None),
        P("expert", "dp", None),
        P("expert", "dp", None),
        P("expert", "dp", None),
    )
    return jax.shard_map(
        on_device, mesh=mesh, in_specs=in_specs, out_specs=out_specs, check_vma=False
    )
```

profile of v0, /device:TPU:1, one launch (start us, length us, event | category | flops | bytes accessed | tf_op | source)
XLA Modules:
  0.0 598.3 jit_solution(11144476672223574724)
XLA Ops:
  10.0 3.6 gather_fusion
  13.7 3.6 gather_fusion.1
  17.9 5.1 select_multiply_fusion.1
  23.0 62.3 %all_to_all.13 = f32[8,96,1024]{2,1,0:T(8,128)} all-to-all(f32[8,96,1024]{2,1,0:T(8,128)S(1)} %get-tuple-element.29), channel_id=1, replica_groups=mesh['dp'=32,'expert'=8] {'expert'}, dimensions={0} | all-to-all | bytes 6291456 | tf_op jit(solution)/shard_map/all_to_all | solution.py:53
  85.3 4.4 all-to-all-start
  89.8 14.5 %convolution_bitcast_fusion.1 = f32[1024,1024]{0,1:T(8,128)} fusion(f32[8,96,1024]{2,1,0:T(8,128)} %all_to_all.13), kind=kOutput, calls=%fused_computation.22 | convolution fusion | flops 9663676416 | bytes 7340032 | tf_op jit(solution)/shard_map/rc,rf->cf/dot_general | solution.py:12
  104.2 29.1 %all-to-all-done = f32[8,96,1024]{2,1,0:T(8,128)} async-done(((f32[8,96,1024]{2,1,0:T(8,128)}), f32[8,96,1024]{2,1,0:T(8,128)}, u32[]{:S(2)}, u32[]{:S(2)}) %all-to-all-start) | async-done | bytes 3145760 | tf_op jit(solution)/shard_map/all_to_all | solution.py:52
  133.4 13.0 %convolution_bitcast_fusion = f32[1024,1024]{0,1:T(8,128)S(1)} fusion(f32[8,96,1024]{2,1,0:T(8,128)} %all_to_all.13, f32[8,96,1024]{2,1,0:T(8,128)} %all-to-all-done), kind=kOutput, calls=%fused_computation.21 | convolution fusion | flops 9663676416 | bytes 10485760 | tf_op jit(solution)/shard_map/rc,rf->cf/dot_general | solution.py:12
  146.4 13.4 %convolution_bitcast_fusion.2 = f32[1024,1024]{0,1:T(8,128)S(1)} fusion(f32[8,96,1024]{2,1,0:T(8,128)} %all-to-all-done), kind=kOutput, calls=%fused_computation.23 | convolution fusion | flops 9663676416 | bytes 7340032 | tf_op jit(solution)/shard_map/rc,rf->cf/dot_general | solution.py:12
  159.8 5.6 pad_maximum_fusion
  165.4 12.6 %copy.56 = f32[1024,3072]{1,0:T(8,128)} copy(f32[1024,3072]{0,1:T(8,128)} %pad_maximum_fusion) | data formatting | bytes 25165824
  178.0 9.5 %all-to-all-start.2 = ((f32[8,1,96]{2,1,0:T(1,128)}), f32[8,1,96]{2,1,0:T(1,128)S(1)}, u32[]{:S(2)}, u32[]{:S(2)}) async-start(f32[8,1,96]{2,1,0:T(1,128)} %bitcast.11), calls=%async_computation.2 | async-start | bytes 8192 | tf_op jit(solution)/shard_map/all_to_all | solution.py:54
  187.8 8.6 %all-to-all-done.2 = f32[8,1,96]{2,1,0:T(1,128)S(1)} async-done(((f32[8,1,96]{2,1,0:T(1,128)}), f32[8,1,96]{2,1,0:T(1,128)S(1)}, u32[]{:S(2)}, u32[]{:S(2)}) %all-to-all-start.2) | async-done | bytes 3104 | tf_op jit(solution)/shard_map/all_to_all | solution.py:54
  197.0 92.2 %psum.7 = f32[1]{0:T(128)} all-reduce(f32[1]{0:T(128)} %bitcast.12), channel_id=1, replica_groups=mesh['dp'=32,'expert'=8] {'dp'}, use_global_device_ids=true, to_apply=%region_7.9 | all-reduce | flops 1 | bytes 8 | tf_op jit(solution)/shard_map/psum | solution.py:56
  289.8 90.7 %reduce-scatter.4.cloned.1.call-done = f32[32,3072]{1,0:T(8,128)} async-done(((f32[1024,3072]{1,0:T(8,128)}), f32[32,3072]{1,0:T(8,128)}) %reduce-scatter.4.cloned.1.call-update) | async-done | bytes 393232
  387.1 60.9 %all-gather.7.cloned.1.call-done = f32[1,1024,1024]{2,0,1:T(1,128)} async-done(((f32[1,32,1024]{2,0,1:T(1,128)}), f32[1,1024,1024]{2,0,1:T(1,128)}) %all-gather.7.cloned.1.call-update) | async-done | bytes 4194320 | tf_op jit(solution)/shard_map/all_gather | solution.py:72
  451.6 60.8 %all-gather.5.cloned.1.call-done = f32[1,1024,1024]{2,0,1:T(1,128)} async-done(((f32[1,32,1024]{2,0,1:T(1,128)}), f32[1,1024,1024]{2,0,1:T(1,128)}) %all-gather.5.cloned.1.call-update) | async-done | bytes 4194320 | tf_op jit(solution)/shard_map/all_gather | solution.py:73
  516.0 3.1 abs_reduce_fusion
  519.7 3.1 abs_reduce_fusion.1
  524.7 3.4 fusion
  533.5 43.0 %all-gather.9.cloned.1.call-done = f32[1024,1024]{1,0:T(8,128)} async-done(((f32[32,1024]{1,0:T(8,128)}), f32[1024,1024]{1,0:T(8,128)}) %all-gather.9.cloned.1.call-update) | async-done | bytes 4194320 | tf_op jit(solution)/shard_map/all_gather | solution.py:74
  576.6 4.8 fusion.38
  581.4 3.3 fusion.6
  587.6 3.0 fusion.21
  (65 shorter events, 27.0 us)
Async XLA Ops:
  7.2 2.8 copy-start
  10.0 3.7 copy-start.2
  85.3 48.1 %all-to-all-start = ((f32[8,96,1024]{2,1,0:T(8,128)}), f32[8,96,1024]{2,1,0:T(8,128)}, u32[]{:S(2)}, u32[]{:S(2)}) async-start(f32[8,96,1024]{2,1,0:T(8,128)} %get-tuple-element.28), calls=%async_computation | async-start | bytes 6291456 | tf_op jit(solution)/shard_map/all_to_all | solution.py:52
  89.7 290.8 %reduce-scatter.4.cloned.1.call-start = ((), (), s32[]{:S(2)}) async-start(), calls=%async_computation.7 | async-start | bytes 12976128
  146.4 13.4 %copy-start.5 = (f32[1024,1024]{0,1:T(8,128)S(1)}, f32[1024,1024]{0,1:T(8,128)}, u32[]{:S(2)}) copy-start(f32[1024,1024]{0,1:T(8,128)} %convolution_bitcast_fusion.1) | copy-start | bytes 12582916
  178.0 9.6 %copy-start.6 = (f32[1,32,1024]{2,1,0:T(8,128)S(1)}, f32[1,32,1024]{2,1,0:T(8,128)}, u32[]{:S(2)}) copy-start(f32[1,32,1024]{2,1,0:T(8,128)} %param.14) | copy-start | bytes 393220
  178.0 204.7 %copy-start.7 = (f32[1,32,1024]{2,1,0:T(8,128)S(1)}, f32[1,32,1024]{2,1,0:T(8,128)}, u32[]{:S(2)}) copy-start(f32[1,32,1024]{2,1,0:T(8,128)} %param.15) | copy-start | bytes 393220
  178.0 18.3 %all-to-all-start.2 = ((f32[8,1,96]{2,1,0:T(1,128)}), f32[8,1,96]{2,1,0:T(1,128)S(1)}, u32[]{:S(2)}, u32[]{:S(2)}) async-start(f32[8,1,96]{2,1,0:T(1,128)} %bitcast.11), calls=%async_computation.2 | async-start | bytes 8192 | tf_op jit(solution)/shard_map/all_to_all | solution.py:54
  187.5 260.5 %all-gather.7.cloned.1.call-start = ((), (), s32[]{:S(2)}) async-start(), calls=%async_computation.5 | async-start | bytes 4325376 | tf_op jit(solution)/shard_map/all_gather | solution.py:72
  382.7 129.7 %all-gather.5.cloned.1.call-start = ((), (), s32[]{:S(2)}) async-start(), calls=%async_computation.4 | async-start | bytes 4325376 | tf_op jit(solution)/shard_map/all_gather | solution.py:73
  384.1 192.5 %all-gather.9.cloned.1.call-start = ((), (), s32[]{:S(2)}) async-start(), calls=%async_computation.6 | async-start | bytes 4325376 | tf_op jit(solution)/shard_map/all_gather | solution.py:74
  524.7 3.5 copy-start.3
  576.6 4.8 copy-start.4
  584.7 2.9 copy-start.10
  584.7 6.7 %copy-start.1 = (f32[256,1024]{1,0:T(8,128)S(1)}, f32[256,1024]{1,0:T(8,128)}, u32[]{:S(2)}) copy-start(f32[256,1024]{1,0:T(8,128)} %param.10) | copy-start | bytes 3145732
  587.6 3.0 copy-start.8
  590.7 0.7 copy-start.9
Sparse Core Ops, SparseCore 0:
  178.1 202.3 reduce-scatter.3
  382.8 65.2 all-gather.6
  450.5 61.8 all-gather.4
  514.7 61.8 all-gather.8
where the time goes:
time: 605 us; the launch traced here: 598 us
  waiting for transfers between devices  293 us (48%)
  blocking collectives  154 us (25%)
  matrix products  60.3 us (10%)
  other arithmetic  32 us (5%)
  local copies, waits for them, and re-layouts  26.4 us (4%)
  between operations  17.8 us (3%)
  starting transfers between devices  14.3 us (2%)
    psum x1, blocking collectives, on_device(): mine = lax.psum(jnp.sum(got_present, axis=1), 'dp')  92.2 us
    unnamed x5, waiting for transfers between devices  90.7 us
    all_to_all x1, blocking collectives, on_device(): lax.all_to_all(sent_grads, 'expert', split_axis=0, concat_axis=1, tiled=T...  62.3 us
    all_gather x1, waiting for transfers between devices, on_device(): lax.all_gather(act_factor, 'dp', axis=1, tiled=True)  60.9 us
    all_gather x1, waiting for transfers between devices, on_device(): lax.all_gather(grad_factor, 'dp', axis=1, tiled=True)  60.8 us
    all_gather x1, waiting for transfers between devices, on_device(): lax.all_gather(gradient_rows, 'dp', axis=1, tiled=True)  43 us
    dot_general x3, matrix products, inner_rows(): jnp.einsum('rc,rf->cf', left, right, precision=lax.Precision.HIGHEST, pre...  40.9 us
    all_to_all x1, waiting for transfers between devices, on_device(): lax.all_to_all(sent_acts, 'expert', split_axis=0, concat_axis=1, tiled=True)  29.1 us
  transfers between devices with their start and end apart: 6, of which 6 were waited for; matrix products, arithmetic and copies ran while one was open for 7% of the time, Pallas kernels for 0%

commit v1 on v0

v1 whole, which is shorter than its diff:
```python
import jax
import jax.numpy as jnp
from jax import lax
from jax.experimental import pallas as pl
from jax.experimental.pallas import tpu as pltpu
from jax.sharding import PartitionSpec as P

MESH = pl.DeviceIdType.MESH
F32 = jnp.float32
BF16 = jnp.bfloat16
ROWS = 256
FEAT = 1024
CAP = 96
WIN = 640
EXT = 1536
SUM_COLS = ((0, 768), (768, 640), (1408, 1024))
SUM_W = 2432
ALL_COLS = ((0, 640), (640, 640), (1280, 1024))
ALL_W = 2304


def coords():
    dp = lax.axis_index("dp")
    ex = lax.axis_index("expert")
    c = lax.rem(dp, 2)
    x = lax.rem(lax.div(dp, 2), 4)
    zl = lax.div(dp, 8)
    y = lax.rem(ex, 4)
    zh = lax.div(ex, 4)
    return x, y, zl, zh, c


def device(x, y, z, c):
    return (lax.rem(z, 4) * 8 + x * 2 + c, lax.div(z, 4) * 4 + y)


def remote(src, dst, send, recv, dev):
    return pltpu.make_async_remote_copy(
        src_ref=src, dst_ref=dst, send_sem=send, recv_sem=recv, device_id=dev, device_id_type=MESH
    )


def dot(a, b):
    return jnp.dot(a, b, preferred_element_type=F32)


def dot_t(a, b):
    return lax.dot_general(a, b, (((0,), (0,)), ((), ())), preferred_element_type=F32)


def split(v):
    hi = v.astype(BF16)
    return hi, (v - hi.astype(F32)).astype(BF16)


def gather_kernel(
    acts, grads, pos, out, raw_a, raw_g, posb, pkh, pkl,
    loc, s_y, r_y, s_f, r_f, s_p, r_p, s_q, r_q,
):
    x, y, zl, zh, c = coords()
    z = zh * 4 + zl
    up, down, far = lax.rem(y + 1, 4), lax.rem(y + 3, 4), lax.rem(y + 2, 4)
    d_up, d_down, d_mate = device(x, up, z, c), device(x, down, z, c), device(x, y, z, 1 - c)
    peers = [
        d_up, d_down, device(x, far, z, c), d_mate,
        device(x, up, z, 1 - c), device(x, down, z, 1 - c), device(x, far, z, 1 - c),
    ]
    barrier = pltpu.get_barrier_semaphore()
    for peer in peers:
        pl.semaphore_signal(barrier, inc=1, device_id=peer, device_id_type=MESH)
    pl.semaphore_wait(barrier, 7)

    src = (acts, grads)
    raw = (raw_a, raw_g)

    def piece(t, slot, half):
        return raw[t].at[pl.ds(slot * ROWS + half * 128, 128), :]

    def own(t, half):
        return src[t].at[pl.ds(half * 128, 128), :]

    started = []

    def go(cp):
        cp.start()
        started.append(cp)

    locals_ = [
        pltpu.make_async_copy(src[t], raw[t].at[pl.ds(0, ROWS), :], loc.at[t]) for t in range(2)
    ]
    locals_.append(pltpu.make_async_copy(pos, posb.at[0], loc.at[2]))
    for cp in locals_:
        cp.start()
    toward = (d_up, d_down)
    direct, forward, mate = {}, {}, {}
    for t in range(2):
        for turn in range(2):
            for way in range(2):
                half = turn ^ way
                direct[way, t, half] = remote(
                    own(t, half), piece(t, 1 + way, half), s_y.at[way, t, half],
                    r_y.at[way, t, half], toward[way],
                )
                go(direct[way, t, half])
        for half in range(2):
            mate[0, t, half] = remote(
                own(t, half), piece(t, 4, half), s_p.at[0, t, half], r_p.at[0, t, half], d_mate
            )
            go(mate[0, t, half])
        if t == 0:
            quick = []
            for i, peer in enumerate(peers):
                quick.append(
                    remote(pos, posb.at[i + 1], s_q.at[i + 1], r_q.at[i + 1], peer)
                )
                go(quick[-1])

    def relay(slot, t, half):
        mate[slot, t, half] = remote(
            piece(t, slot, half), piece(t, 4 + slot, half), s_p.at[slot, t, half],
            r_p.at[slot, t, half], d_mate,
        )
        go(mate[slot, t, half])

    lane = c * 4 + y
    slot_ids = lax.broadcasted_iota(jnp.int32, (CAP, ROWS), 0)

    def pack(t):
        def body(s, carry):
            row = posb[s, pl.ds(lane, 1), :]
            sel = jnp.where(slot_ids == row, F32(1.0), F32(0.0)).astype(BF16)
            at = pl.ds(pl.multiple_of(s * CAP, CAP), CAP)
            for cb in range(4):
                v = raw[t][pl.ds(pl.multiple_of(s * ROWS, ROWS), ROWS), cb * 256:(cb + 1) * 256]
                hi, lo = split(v)
                for part, dest in ((hi, pkh), (lo, pkl)):
                    got = dot(sel, part).astype(BF16)
                    base = t * EXT + cb * 256
                    dest[at, base:base + 256] = got
                    if cb < 2:
                        dest[at, base + FEAT:base + FEAT + 256] = got
            return carry

        lax.fori_loop(0, 8, body, 0)

    def gram(lhs, rhs, width, store):
        def body(ib, carry):
            at = pl.multiple_of(ib * 256, 256)
            lh = pkh[:, pl.ds(lhs + at, 256)]
            ll = pkl[:, pl.ds(lhs + at, 256)]
            for nb in range(width // 256):
                begin = rhs(at) + nb * 256
                rh = pkh[:, pl.ds(begin, 256)]
                rl = pkl[:, pl.ds(begin, 256)]
                store(at, nb, dot_t(lh, rh) + (dot_t(lh, rl) + dot_t(ll, rh)))
            return carry

        lax.fori_loop(0, 4, body, 0)

    def window_store(first):
        def store(at, nb, acc):
            top, bottom = pl.ds(at, 128), pl.ds(at + 128, 128)
            lo, hi = nb * 256, nb * 256 + 256
            keep = min(hi, WIN)
            out[top, first + lo:first + keep] = acc[:128, :keep - lo]
            begin = max(lo - 128, 0)
            out[bottom, first + begin:first + hi - 128] = acc[128:, begin + 128 - lo:]
        return store

    def cross_store(at, nb, acc):
        out[pl.ds(at, 256), 1408 + nb * 256:1408 + nb * 256 + 256] = acc

    for cp in locals_:
        cp.wait()
    for t in range(2):
        for turn in range(2):
            for way in range(2):
                half = turn ^ way
                direct[way, t, half].wait_recv()
                if turn == 0:
                    forward[way, t] = remote(
                        piece(t, 1 + way, half), piece(t, 3, half), s_f.at[way, t],
                        r_f.at[way, t], toward[way],
                    )
                    go(forward[way, t])
                relay(1 + way, t, half)
        for way in range(2):
            forward[way, t].wait_recv()
            relay(3, t, way)
        if t == 0:
            for cp in quick:
                cp.wait_recv()
            held = jnp.zeros((8, ROWS), F32)
            for s in range(8):
                row = posb[s, pl.ds(lane, 1), :]
                held = held + jnp.where(row >= 0, F32(1.0), F32(0.0))
            count = jnp.sum(held[0:1, :])
            out[:, 640:768] = jnp.full((FEAT, 128), count, F32)
        for slot in range(4):
            for half in range(2):
                mate[slot, t, half].wait_recv()
        pack(t)
        gram(t * EXT, lambda at, t=t: t * EXT + at, 768, window_store(SUM_COLS[t][0]))
    gram(EXT, lambda at: 0, FEAT, cross_store)
    for cp in started:
        cp.wait_send()


def reduce_kernel(
    part, old_a, old_g, mom, wts, out_a, out_g, out_m, out_w,
    x1, x2a, x2b, acc, z4p, z4m, zp, zm, fin, shard, full, ext, fac, mh, ml,
    s_x, r_x, s_z, r_z, s_c, r_c, s_gz, r_gz, s_gx, r_gx, s_gc, r_gc,
):
    x, y, zl, zh, c = coords()
    z = zh * 4 + zl
    right, left, opp = lax.rem(x + 1, 4), lax.rem(x + 3, 4), lax.rem(x + 2, 4)
    d_right, d_left = device(right, y, z, c), device(left, y, z, c)
    d_up, d_down = device(x, y, lax.rem(z + 1, 8), c), device(x, y, lax.rem(z + 7, 8), c)
    d_mate = device(x, y, z, 1 - c)
    barrier = pltpu.get_barrier_semaphore()
    for peer in (d_right, d_left, d_up, d_down, d_mate):
        pl.semaphore_signal(barrier, inc=1, device_id=peer, device_id_type=MESH)
    pl.semaphore_wait(barrier, 5)

    home = zh == c
    sides = (d_right, d_left)
    near = (right, left)
    lo_half, hi_half = pl.ds(0, 32), pl.ds(32, 32)
    trav, rest = (lo_half, hi_half), (hi_half, lo_half)

    def cols(p):
        return pl.ds(SUM_COLS[p][0], SUM_COLS[p][1])

    def copy_x(p, way, kind):
        if kind == 0:
            s, d = part.at[:, opp, trav[way], cols(p)], x1.at[way, :, :, cols(p)]
        elif kind == 1:
            s, d = part.at[:, near[way], rest[way], cols(p)], x2b.at[way, :, :, cols(p)]
        else:
            s, d = x1.at[way, :, :, cols(p)], x2a.at[way, :, :, cols(p)]
        return remote(s, d, s_x.at[p, way, kind], r_x.at[p, way, kind], sides[way])

    def x_send(p, kind):
        for way in range(2):
            copy_x(p, way, kind).start()

    def x_relay(p):
        for way in range(2):
            copy_x(p, way, 0).wait_recv()

            def body(b, carry):
                x1[way, b, :, cols(p)] = x1[way, b, :, cols(p)] + part[b, near[way], trav[way], cols(p)]
                return carry

            lax.fori_loop(0, 4, body, 0)
        x_send(p, 2)

    def x_final(p):
        for way in range(2):
            copy_x(p, way, 1).wait_recv()
            copy_x(p, way, 2).wait_recv()

        def body(b, carry):
            acc[b, lo_half, cols(p)] = part[b, x, lo_half, cols(p)] + (
                x2a[0, b, :, cols(p)] + x2b[1, b, :, cols(p)])
            acc[b, hi_half, cols(p)] = part[b, x, hi_half, cols(p)] + (
                x2a[1, b, :, cols(p)] + x2b[0, b, :, cols(p)])
            return carry

        lax.fori_loop(0, 4, body, 0)

    z_sides = (d_up, d_down)
    z4 = (z4p, z4m)
    zz = (zp, zm)

    def target(way, k):
        zd = lax.rem(z + k, 8) if way == 0 else lax.rem(z + 8 - k, 8)
        return lax.rem(zd, 4), lax.div(zd, 4) == c

    def copy_z(p, way, kind):
        k = (4, 3, 3, 2, 1)[kind]
        b, _ = target(way, k)
        if kind == 0:
            s, d = acc.at[b, trav[way], cols(p)], z4[way].at[:, cols(p)]
        elif kind == 1:
            s, d = z4[way].at[:, cols(p)], zz[way].at[0, trav[way], cols(p)]
        elif kind == 2:
            s, d = acc.at[b, rest[way], cols(p)], zz[way].at[0, rest[way], cols(p)]
        elif kind == 3:
            s, d = zz[way].at[0, :, cols(p)], zz[way].at[1, :, cols(p)]
        else:
            s, d = zz[way].at[1, :, cols(p)], zz[way].at[2, :, cols(p)]
        return remote(s, d, s_z.at[p, way, kind], r_z.at[p, way, kind], z_sides[way])

    def z_first(p):
        for way in range(2):
            @pl.when(target(way, 4)[1])
            def _(way=way):
                copy_z(p, way, 0).start()

            @pl.when(target(way, 3)[1])
            def _(way=way):
                copy_z(p, way, 2).start()

    def z_step(p, k):
        for way in range(2):
            @pl.when(target(way, k)[1])
            def _(way=way):
                b, _ = target(way, k)
                if k == 3:
                    copy_z(p, way, 0).wait_recv()
                    z4[way][:, cols(p)] = z4[way][:, cols(p)] + acc[b, trav[way], cols(p)]
                    copy_z(p, way, 1).start()
                else:
                    got = 2 - k
                    if k == 2:
                        copy_z(p, way, 1).wait_recv()
                        copy_z(p, way, 2).wait_recv()
                    else:
                        copy_z(p, way, 3).wait_recv()
                    zz[way][got, :, cols(p)] = zz[way][got, :, cols(p)] + acc[b, :, cols(p)]
                    copy_z(p, way, 5 - k).start()

    def copy_c(p):
        return remote(
            acc.at[zl, pl.ds((1 - c) * 32, 32), cols(p)], fin.at[:, cols(p)], s_c.at[p], r_c.at[p], d_mate
        )

    def z_final(p):
        @pl.when(home)
        def _():
            copy_z(p, 0, 4).wait_recv()
            copy_z(p, 1, 4).wait_recv()
            acc[zl, :, cols(p)] = acc[zl, :, cols(p)] + (zp[2, :, cols(p)] + zm[2, :, cols(p)])
            copy_c(p).start()
            fin[:, cols(p)] = acc[zl, pl.ds(c * 32, 32), cols(p)]

    olds = (old_a, old_g)
    block = zl * 2 + lax.div(x, 2)

    def make_shard(p):
        @pl.when(jnp.logical_not(home))
        def _():
            copy_c(p).wait_recv()
        total = jnp.maximum(fin[0:1, 640:641], F32(1.0))
        at = ALL_COLS[p]
        if p < 2:
            ext[:, 0:FEAT] = olds[p][0]
            ext[:, FEAT:EXT] = olds[p][0, :, 0:EXT - FEAT]
            old = ext[:, pl.ds(pl.multiple_of(block * 128, 128), WIN)]
            begin = SUM_COLS[p][0]
            shard[:, at[0]:at[0] + WIN] = 0.5 * old + 0.5 * (fin[:, begin:begin + WIN] / total)
        else:
            begin = SUM_COLS[p][0]
            shard[:, at[0]:at[0] + FEAT] = fin[:, begin:begin + FEAT] / total
        full[zl, x, c, :, at[0]:at[0] + at[1]] = shard[:, at[0]:at[0] + at[1]]

    def acols(p):
        return pl.ds(ALL_COLS[p][0], ALL_COLS[p][1])

    def copy_gz(p, way, step):
        origin = zl - (step - 1) if way == 0 else zl + (step - 1)
        ok = jnp.logical_and(origin >= 0, zl < 3) if way == 0 else jnp.logical_and(origin <= 3, zl > 0)
        ref = full.at[jnp.clip(origin, 0, 3), x, c, :, acols(p)]
        s = shard.at[:, acols(p)] if step == 1 else ref
        return ok, remote(s, ref, s_gz.at[p, way, step - 1], r_gz.at[p, way, step - 1], z_sides[way])

    def gz_send(p, step):
        for way in range(2):
            ok, cp = copy_gz(p, way, step)
            @pl.when(ok)
            def _(cp=cp):
                cp.start()

    def gz_wait(p, step):
        for way in range(2):
            ok = zl - step >= 0 if way == 0 else zl + step <= 3
            cp = copy_gz(p, way, step)[1]
            @pl.when(ok)
            def _(cp=cp):
                cp.wait_recv()

    def copy_gx(p, way, kind):
        if kind == 0:
            ref = full.at[:, x, c, :, acols(p)]
        else:
            who = left if way == 0 else right
            ref = full.at[:, who, c, pl.ds(16 * way, 16), acols(p)]
        return remote(ref, ref, s_gx.at[p, way, kind], r_gx.at[p, way, kind], sides[way])

    def copy_gc(p, i):
        who = (x, left, right, opp)[i]
        ref = full.at[:, who, c, :, acols(p)]
        return remote(ref, ref, s_gc.at[p, i], r_gc.at[p, i], d_mate)

    def gx_send(p):
        for way in range(2):
            copy_gx(p, way, 0).start()
        copy_gc(p, 0).start()

    def gx_forward(p):
        for way in range(2):
            copy_gx(p, way, 0).wait_recv()
            copy_gx(p, way, 1).start()
            copy_gc(p, 1 + way).start()

    def gx_last(p):
        for way in range(2):
            copy_gx(p, way, 1).wait_recv()
        copy_gc(p, 3).start()

    def g_wait(p):
        for i in range(4):
            copy_gc(p, i).wait_recv()

    x_send(0, 0)
    x_send(0, 1)
    x_send(1, 0)
    x_relay(0)
    x_send(1, 1)
    x_send(2, 0)
    x_relay(1)
    x_final(0)
    z_first(0)
    x_send(2, 1)
    x_relay(2)
    z_step(0, 3)
    x_final(1)
    z_first(1)
    z_step(0, 2)
    z_step(1, 3)
    z_step(0, 1)
    x_final(2)
    z_first(2)
    z_step(1, 2)
    z_final(0)
    z_step(2, 3)
    z_step(1, 1)
    make_shard(0)
    gz_send(0, 1)
    z_step(2, 2)
    z_final(1)
    z_step(2, 1)
    gz_wait(0, 1)
    gz_send(0, 2)
    make_shard(1)
    gz_send(1, 1)
    z_final(2)
    gz_wait(0, 2)
    gz_send(0, 3)
    make_shard(2)
    gz_send(2, 1)
    gz_wait(1, 1)
    gz_send(1, 2)
    gz_wait(0, 3)
    gx_send(0)
    gz_wait(2, 1)
    gz_send(2, 2)
    gz_wait(1, 2)
    gz_send(1, 3)
    gz_wait(2, 2)
    gz_send(2, 3)
    gz_wait(1, 3)
    gx_forward(0)
    gx_send(1)
    gz_wait(2, 3)
    gx_last(0)
    gx_forward(1)
    gx_send(2)
    gx_last(1)
    gx_forward(2)

    row_ids = lax.broadcasted_iota(jnp.int32, (128, FEAT), 0)
    col_ids = lax.broadcasted_iota(jnp.int32, (128, FEAT), 1)
    alphas, damps = [], []
    for t in range(2):
        g_wait(t)
        first = ALL_COLS[t][0]

        def rows_of(i, first_col):
            b, h = lax.div(i, 2), lax.rem(i, 2)
            got = full[b, pl.ds(h * 2, 2), :, :, first_col]
            return got.reshape(128, 128)

        def build(i, tr, t=t, first=first):
            at = pl.ds(pl.multiple_of(i * 128, 128), 128)
            for k in range(8):
                j = lax.rem(i + k, 8)
                if k <= 4:
                    blk = rows_of(i, pl.ds(first + k * 128, 128))
                else:
                    blk = rows_of(j, pl.ds(first + (8 - k) * 128, 128)).T
                if k == 0:
                    tr = tr + jnp.sum(jnp.where(row_ids[:, :128] == col_ids[:, :128], blk, F32(0.0)))
                fac[t, at, pl.ds(pl.multiple_of(j * 128, 128), 128)] = blk
            return tr

        trace = lax.fori_loop(0, 8, build, F32(0.0))
        damp = F32(0.1) * trace / F32(FEAT)

        def shift(i, best, t=t, damp=damp):
            at = pl.ds(pl.multiple_of(i * 128, 128), 128)
            m = fac[t, at, :] + jnp.where(row_ids + i * 128 == col_ids, damp, F32(0.0))
            hi, lo = split(m)
            mh[t, at, :] = hi
            ml[t, at, :] = lo
            return jnp.maximum(best, jnp.max(jnp.sum(jnp.abs(m), axis=1, keepdims=True)))

        best = lax.fori_loop(0, 8, shift, F32(0.0))
        alphas.append(F32(1.0) / jnp.full((1, 1), best, F32))
        damps.append(damp)
        if t == 0:
            gx_last(2)

    d = zl * 8 + x * 2 + c
    mine = pl.ds(pl.multiple_of(d * 32, 32), 32)
    out_a[0] = fac[0, mine, :]
    out_g[0] = fac[1, mine, :]

    def times(v, t):
        hi, lo = split(v)
        both = jnp.concatenate([hi, lo], axis=0)
        parts = []
        for nb in range(4):
            at = slice(nb * 256, nb * 256 + 256)
            one = dot(both, mh[t, :, at])
            parts.append(one[:32] + (one[32:] + dot(hi, ml[t, :, at])))
        return jnp.concatenate(parts, axis=1)

    aa, ag = alphas
    unit_rows = jnp.where(
        lax.broadcasted_iota(jnp.int32, (32, FEAT), 0) + d * 32
        == lax.broadcasted_iota(jnp.int32, (32, FEAT), 1), F32(1.0), F32(0.0))
    shifted_rows = fac[1, mine, :] + damps[1] * unit_rows
    u1 = ag * (2.0 * unit_rows - ag * shifted_rows)
    u2 = times(u1, 1)
    inv_rows = 2.0 * u1 - ag * (2.0 * u2 - ag * times(u2, 1))
    g_wait(2)
    hi, lo = split(inv_rows)
    both = jnp.concatenate([hi, lo], axis=0)
    parts = []
    for nb in range(4):
        rh, rl = split(full[:, :, :, :, 1280 + nb * 256:1536 + nb * 256].reshape(FEAT, 256))
        one = dot(both, rh)
        parts.append(one[:32] + (one[32:] + dot(hi, rl)))
    lhs = jnp.concatenate(parts, axis=1)
    half_way = aa * (2.0 * lhs - aa * times(lhs, 0))
    w = times(half_way, 0)
    precond = 2.0 * half_way - aa * (2.0 * w - aa * times(w, 0))
    moment = 0.9 * mom[0] + precond
    out_m[0] = moment
    out_w[0] = wts[0] - 0.5 * moment

    for p in range(3):
        for way in range(2):
            for kind in range(3):
                copy_x(p, way, kind).wait_send()
            for kind in range(5):
                k = (4, 3, 3, 2, 1)[kind]
                @pl.when(target(way, k)[1])
                def _(p=p, way=way, kind=kind):
                    copy_z(p, way, kind).wait_send()
            for step in range(1, 4):
                ok, cp = copy_gz(p, way, step)
                @pl.when(ok)
                def _(cp=cp):
                    cp.wait_send()
            for kind in range(2):
                copy_gx(p, way, kind).wait_send()
        @pl.when(home)
        def _(p=p):
            copy_c(p).wait_send()
        for i in range(4):
            copy_gc(p, i).wait_send()


def on_device(acts, grads_out, routes, counts, old_act_factor, old_grad_factor, momentum, weights):
    experts = jnp.arange(8, dtype=jnp.int32)
    hit = jnp.sum(
        (routes.T[:, None, :] == experts[None, :, None]).astype(jnp.int32), axis=0, dtype=jnp.int32
    )
    rank = jnp.cumsum(hit, axis=1, dtype=jnp.int32) - hit
    kept = (hit > 0) & (rank < counts[0][:, None])
    pos = jnp.where(kept, rank, -1)
    vm = pl.BlockSpec(memory_space=pltpu.VMEM)
    hbm = pl.BlockSpec(memory_space=pl.ANY)
    dma = pltpu.SemaphoreType.DMA
    sums = pl.pallas_call(
        gather_kernel,
        out_shape=jax.ShapeDtypeStruct((FEAT, SUM_W), F32),
        in_specs=[hbm, hbm, hbm],
        out_specs=vm,
        scratch_shapes=[
            pltpu.VMEM((8 * ROWS, FEAT), F32),
            pltpu.VMEM((8 * ROWS, FEAT), F32),
            pltpu.VMEM((8, 8, ROWS), jnp.int32),
            pltpu.VMEM((8 * CAP, 2 * EXT), BF16),
            pltpu.VMEM((8 * CAP, 2 * EXT), BF16),
            dma((3,)), dma((2, 2, 2)), dma((2, 2, 2)), dma((2, 2)), dma((2, 2)),
            dma((4, 2, 2)), dma((4, 2, 2)), dma((8,)), dma((8,)),
        ],
        compiler_params=pltpu.CompilerParams(
            collective_id=0, has_side_effects=True, vmem_limit_bytes=60 * 1024 * 1024
        ),
        name="gather_rows",
    )(acts, grads_out, pos)
    out = jax.ShapeDtypeStruct((1, 32, FEAT), F32)
    return pl.pallas_call(
        reduce_kernel,
        out_shape=(out, out, out, out),
        in_specs=[vm] * 5,
        out_specs=[vm] * 4,
        scratch_shapes=[
            pltpu.VMEM((2, 4, 32, SUM_W), F32),
            pltpu.VMEM((2, 4, 32, SUM_W), F32),
            pltpu.VMEM((2, 4, 32, SUM_W), F32),
            pltpu.VMEM((4, 64, SUM_W), F32),
            pltpu.VMEM((32, SUM_W), F32),
            pltpu.VMEM((32, SUM_W), F32),
            pltpu.VMEM((3, 64, SUM_W), F32),
            pltpu.VMEM((3, 64, SUM_W), F32),
            pltpu.VMEM((32, SUM_W), F32),
            pltpu.VMEM((32, ALL_W), F32),
            pltpu.VMEM((4, 4, 2, 32, ALL_W), F32),
            pltpu.VMEM((32, EXT), F32),
            pltpu.VMEM((2, FEAT, FEAT), F32),
            pltpu.VMEM((2, FEAT, FEAT), BF16),
            pltpu.VMEM((2, FEAT, FEAT), BF16),
            dma((3, 2, 3)), dma((3, 2, 3)), dma((3, 2, 5)), dma((3, 2, 5)), dma((3,)), dma((3,)),
            dma((3, 2, 3)), dma((3, 2, 3)), dma((3, 2, 2)), dma((3, 2, 2)), dma((3, 4)), dma((3, 4)),
        ],
        compiler_params=pltpu.CompilerParams(
            collective_id=1, has_side_effects=True, vmem_limit_bytes=63 * 1024 * 1024
        ),
        name="reduce_apply",
    )(sums.reshape(4, 4, 64, SUM_W), old_act_factor, old_grad_factor, momentum, weights)


def solution(mesh):
    rows = P(("dp", "expert"), None)
    mats = P("expert", "dp", None)
    return jax.shard_map(
        on_device,
        mesh=mesh,
        in_specs=(rows, rows, rows, rows, mats, mats, mats, mats),
        out_specs=(mats, mats, mats, mats),
        check_vma=False,
    )
```

time: 605 us -> 289 us (0.48)
  waiting for transfers between devices: 293 us -> 0 us
  Pallas kernels: 0 us -> 278 us
  blocking collectives: 154 us -> 0 us
  matrix products: 60.3 us -> 0 us
  other arithmetic: 32 us -> 2.63 us
  local copies, waits for them, and re-layouts: 26.4 us -> 6.49 us
  between operations: 17.8 us -> 0.65 us
  starting transfers between devices: 14.3 us -> 0 us
    pallas_call x0 -> x2, Pallas kernels: none -> 278 us  [the longest x1 171 us: on_device(): pl.pallas_call(reduce_kernel, out_shape=(out, out, out, out), in_specs=[v...]
    all_gather x3 -> x0, waiting for transfers between devices: 165 us -> none  [the longest x1 60.9 us: on_device(): lax.all_gather(act_factor, 'dp', axis=1, tiled=True)]
    psum x1 -> x0, blocking collectives: 92.2 us -> none  [on_device(): mine = lax.psum(jnp.sum(got_present, axis=1), 'dp')]
    unnamed x5 -> x0, waiting for transfers between devices: 90.7 us -> none
    all_to_all x1 -> x0, blocking collectives: 62.3 us -> none  [on_device(): lax.all_to_all(sent_grads, 'expert', split_axis=0, concat_axis=1, tiled=T...]
    dot_general x9 -> x0, matrix products: 60.3 us -> none  [the longest x3 40.9 us: inner_rows(): jnp.einsum('rc,rf->cf', left, right, precision=lax.Precision.HIGHEST, pre...]
    all_to_all x2 -> x0, waiting for transfers between devices: 37.7 us -> none  [the longest x1 29.1 us: on_device(): lax.all_to_all(sent_acts, 'expert', split_axis=0, concat_axis=1, tiled=True)]
    all_to_all x2 -> x0, starting transfers between devices: 13.9 us -> none  [the longest x1 9.49 us: on_device(): lax.all_to_all(present, 'expert', split_axis=0, concat_axis=1, tiled=True)]
  transfers between devices with their start and end apart: 6 -> 0, of which waited for: 6 -> 0; matrix products, arithmetic and copies ran while one was open for 7% -> 0% of each run, Pallas kernels for 0% -> 0%
where the time goes in v1:
time: 289 us; the launch traced here: 288 us
  Pallas kernels  278 us (96%)
  local copies, waits for them, and re-layouts  6.49 us (2%)
    pallas_call x1, Pallas kernels, on_device(): pl.pallas_call(reduce_kernel, out_shape=(out, out, out, out), in_specs=[v...  171 us
    pallas_call x1, Pallas kernels, on_device(): pl.pallas_call(gather_kernel, out_shape=jax.ShapeDtypeStruct((FEAT, SUM_W...  107 us
    unnamed x4, local copies, waits for them, and re-layouts  6.27 us

profile of v1, /device:TPU:1, one launch (start us, length us, event | category | flops | bytes accessed | tf_op | source)
XLA Modules:
  0.0 287.5 jit_solution(14905838923330256576)
XLA Ops:
  0.6 0.7 convert_reduce_fusion
  1.3 0.6 reduce-window.6
  1.9 0.2 slice_reduce_fusion
  2.1 1.3 and_select_fusion.pos
  3.5 106.5 %gather_rows.1 = f32[1024,2432]{1,0:T(8,128)} custom-call(f32[256,1024]{1,0:T(8,128)} %acts.1, f32[256,1024]{1,0:T(8,128)} %grads.1, s32[8,256]{1,0:T(8,128)} %and_select_fusion.pos), custom_call_target="tpu_custom_call" | custom-call | tf_op jit(solution)/shard_map/gather_rows/pallas_call | solution.py:588
  110.0 171.2 %reduce_apply.1 = (f32[1,32,1024]{2,1,0:T(8,128)}, f32[1,32,1024]{2,1,0:T(8,128)}, f32[1,32,1024]{2,1,0:T(8,128)}, f32[1,32,1024]{2,1,0:T(8,128)}) custom-call(f32[4,4,64,2432]{3,2,1,0:T(8,128)} %bitcast.8, f32[1,32,1024]{2,1,0:T(8,128)} %old_a.1, f32[1,32,1024]{2,1,0:T(8,128)} %old_g.1, f32[1,32,1024]{2,1,0:T(8,128)} %mom.1, f32[1,32,1024]{2,1,0:T(8,128)} %wts.1), custom_call_target="tpu_custom_call" | custom-call | tf_op jit(solution)/shard_map/reduce_apply/pallas_call | solution.py:608
  281.2 1.6 copy.16
  282.8 1.6 copy.17
  284.4 1.6 copy.18
  286.0 1.6 copy.19
  (2 shorter events, 0.0 us)

commit v2 on v1

--- a/solution.py
+++ b/solution.py
@@ -11,6 +11,7 @@
 ROWS = 256
 FEAT = 1024
 CAP = 96
+SLOTS = 8 * CAP
 WIN = 640
 EXT = 1536
 SUM_COLS = ((0, 768), (768, 640), (1408, 1024))
@@ -53,12 +54,18 @@
     return hi, (v - hi.astype(F32)).astype(BF16)
 
 
-def gather_kernel(
-    acts, grads, pos, out, raw_a, raw_g, posb, pkh, pkl,
+def step_kernel(
+    acts, grads, pos, old_a, old_g, out,
+    raw_a, raw_g, posb, pkh, pkl, part,
+    x1, x2a, x2b, z4p, z4m, zp, zm, fin, full, ext,
     loc, s_y, r_y, s_f, r_f, s_p, r_p, s_q, r_q,
+    s_x, r_x, s_z, r_z, s_c, r_c, s_gz, r_gz, s_gx, r_gx, s_gc, r_gc,
 ):
     x, y, zl, zh, c = coords()
     z = zh * 4 + zl
+    right, left, opp = lax.rem(x + 1, 4), lax.rem(x + 3, 4), lax.rem(x + 2, 4)
+    d_right, d_left = device(right, y, z, c), device(left, y, z, c)
+    d_ztop, d_zlow = device(x, y, lax.rem(z + 1, 8), c), device(x, y, lax.rem(z + 7, 8), c)
     up, down, far = lax.rem(y + 1, 4), lax.rem(y + 3, 4), lax.rem(y + 2, 4)
     d_up, d_down, d_mate = device(x, up, z, c), device(x, down, z, c), device(x, y, z, 1 - c)
     peers = [
@@ -66,9 +73,9 @@
         device(x, up, z, 1 - c), device(x, down, z, 1 - c), device(x, far, z, 1 - c),
     ]
     barrier = pltpu.get_barrier_semaphore()
-    for peer in peers:
+    for peer in peers + [d_right, d_left, d_ztop, d_zlow]:
         pl.semaphore_signal(barrier, inc=1, device_id=peer, device_id_type=MESH)
-    pl.semaphore_wait(barrier, 7)
+    pl.semaphore_wait(barrier, 11)
 
     src = (acts, grads)
     raw = (raw_a, raw_g)
@@ -93,7 +100,8 @@
         cp.start()
     toward = (d_up, d_down)
     direct, forward, mate = {}, {}, {}
-    for t in range(2):
+
+    def send_rows(t):
         for turn in range(2):
             for way in range(2):
                 half = turn ^ way
@@ -107,13 +115,12 @@
                 own(t, half), piece(t, 4, half), s_p.at[0, t, half], r_p.at[0, t, half], d_mate
             )
             go(mate[0, t, half])
-        if t == 0:
-            quick = []
-            for i, peer in enumerate(peers):
-                quick.append(
-                    remote(pos, posb.at[i + 1], s_q.at[i + 1], r_q.at[i + 1], peer)
-                )
-                go(quick[-1])
+
+    send_rows(0)
+    quick = []
+    for i, peer in enumerate(peers):
+        quick.append(remote(pos, posb.at[i + 1], s_q.at[i + 1], r_q.at[i + 1], peer))
+        go(quick[-1])
 
     def relay(slot, t, half):
         mate[slot, t, half] = remote(
@@ -143,7 +150,7 @@
 
         lax.fori_loop(0, 8, body, 0)
 
-    def gram(lhs, rhs, width, store):
+    def gram(lhs, rhs, width, store, begin_block, end_block):
         def body(ib, carry):
             at = pl.multiple_of(ib * 256, 256)
             lh = pkh[:, pl.ds(lhs + at, 256)]
@@ -152,75 +159,53 @@
                 begin = rhs(at) + nb * 256
                 rh = pkh[:, pl.ds(begin, 256)]
                 rl = pkl[:, pl.ds(begin, 256)]
-                store(at, nb, dot_t(lh, rh) + (dot_t(lh, rl) + dot_t(ll, rh)))
+                store(ib, nb, dot_t(lh, rh) + (dot_t(lh, rl) + dot_t(ll, rh)))
             return carry
 
-        lax.fori_loop(0, 4, body, 0)
+        lax.fori_loop(begin_block, end_block, body, 0)
 
     def window_store(first):
-        def store(at, nb, acc):
-            top, bottom = pl.ds(at, 128), pl.ds(at + 128, 128)
+        def store(ib, nb, got):
             lo, hi = nb * 256, nb * 256 + 256
             keep = min(hi, WIN)
-            out[top, first + lo:first + keep] = acc[:128, :keep - lo]
+            part[ib, 0:2, :, first + lo:first + keep] = got[:128, :keep - lo].reshape(2, 64, keep - lo)
             begin = max(lo - 128, 0)
-            out[bottom, first + begin:first + hi - 128] = acc[128:, begin + 128 - lo:]
+            part[ib, 2:4, :, first + begin:first + hi - 128] = got[128:, begin + 128 - lo:].reshape(
+                2, 64, hi - 128 - begin)
         return store
 
-    def cross_store(at, nb, acc):
-        out[pl.ds(at, 256), 1408 + nb * 256:1408 + nb * 256 + 256] = acc
-
-    for cp in locals_:
-        cp.wait()
-    for t in range(2):
-        for turn in range(2):
-            for way in range(2):
-                half = turn ^ way
-                direct[way, t, half].wait_recv()
-                if turn == 0:
-                    forward[way, t] = remote(
-                        piece(t, 1 + way, half), piece(t, 3, half), s_f.at[way, t],
-                        r_f.at[way, t], toward[way],
-                    )
-                    go(forward[way, t])
-                relay(1 + way, t, half)
+    def cross_store(ib, nb, got):
+        part[ib, :, :, 1408 + nb * 256:1408 + nb * 256 + 256] = got.reshape(4, 64, 256)
+
+    def factor_gram(t, begin_block, end_block):
+        gram(t * EXT, lambda at: t * EXT + at, 768, window_store(SUM_COLS[t][0]), begin_block, end_block)
+
+    def cross_gram(begin_block, end_block):
+        gram(EXT, lambda at: 0, FEAT, cross_store, begin_block, end_block)
+
+    def first_rows(t):
+        for way in range(2):
+            direct[way, t, way].wait_recv()
+            forward[way, t] = remote(
+                piece(t, 1 + way, way), piece(t, 3, way), s_f.at[way, t], r_f.at[way, t], toward[way]
+            )
+            go(forward[way, t])
+            relay(1 + way, t, way)
+
+    def second_rows(t):
+        for way in range(2):
+            direct[way, t, 1 - way].wait_recv()
+            relay(1 + way, t, 1 - way)
+
+    def last_rows(t):
         for way in range(2):
             forward[way, t].wait_recv()
             relay(3, t, way)
-        if t == 0:
-            for cp in quick:
-                cp.wait_recv()
-            held = jnp.zeros((8, ROWS), F32)
-            for s in range(8):
-                row = posb[s, pl.ds(lane, 1), :]
-                held = held + jnp.where(row >= 0, F32(1.0), F32(0.0))
-            count = jnp.sum(held[0:1, :])
-            out[:, 640:768] = jnp.full((FEAT, 128), count, F32)
+
+    def mate_rows(t):
         for slot in range(4):
             for half in range(2):
                 mate[slot, t, half].wait_recv()
-        pack(t)
-        gram(t * EXT, lambda at, t=t: t * EXT + at, 768, window_store(SUM_COLS[t][0]))
-    gram(EXT, lambda at: 0, FEAT, cross_store)
-    for cp in started:
-        cp.wait_send()
-
-
-def reduce_kernel(
-    part, old_a, old_g, mom, wts, out_a, out_g, out_m, out_w,
-    x1, x2a, x2b, acc, z4p, z4m, zp, zm, fin, shard, full, ext, fac, mh, ml,
-    s_x, r_x, s_z, r_z, s_c, r_c, s_gz, r_gz, s_gx, r_gx, s_gc, r_gc,
-):
-    x, y, zl, zh, c = coords()
-    z = zh * 4 + zl
-    right, left, opp = lax.rem(x + 1, 4), lax.rem(x + 3, 4), lax.rem(x + 2, 4)
-    d_right, d_left = device(right, y, z, c), device(left, y, z, c)
-    d_up, d_down = device(x, y, lax.rem(z + 1, 8), c), device(x, y, lax.rem(z + 7, 8), c)
-    d_mate = device(x, y, z, 1 - c)
-    barrier = pltpu.get_barrier_semaphore()
-    for peer in (d_right, d_left, d_up, d_down, d_mate):
-        pl.semaphore_signal(barrier, inc=1, device_id=peer, device_id_type=MESH)
-    pl.semaphore_wait(barrier, 5)
 
     home = zh == c
     sides = (d_right, d_left)
@@ -261,15 +246,15 @@
             copy_x(p, way, 2).wait_recv()
 
         def body(b, carry):
-            acc[b, lo_half, cols(p)] = part[b, x, lo_half, cols(p)] + (
+            part[b, x, lo_half, cols(p)] = part[b, x, lo_half, cols(p)] + (
                 x2a[0, b, :, cols(p)] + x2b[1, b, :, cols(p)])
-            acc[b, hi_half, cols(p)] = part[b, x, hi_half, cols(p)] + (
+            part[b, x, hi_half, cols(p)] = part[b, x, hi_half, cols(p)] + (
                 x2a[1, b, :, cols(p)] + x2b[0, b, :, cols(p)])
             return carry
 
         lax.fori_loop(0, 4, body, 0)
 
-    z_sides = (d_up, d_down)
+    z_sides = (d_ztop, d_zlow)
     z4 = (z4p, z4m)
     zz = (zp, zm)
 
@@ -281,11 +266,11 @@
         k = (4, 3, 3, 2, 1)[kind]
         b, _ = target(way, k)
         if kind == 0:
-            s, d = acc.at[b, trav[way], cols(p)], z4[way].at[:, cols(p)]
+            s, d = part.at[b, x, trav[way], cols(p)], z4[way].at[:, cols(p)]
         elif kind == 1:
             s, d = z4[way].at[:, cols(p)], zz[way].at[0, trav[way], cols(p)]
         elif kind == 2:
-            s, d = acc.at[b, rest[way], cols(p)], zz[way].at[0, rest[way], cols(p)]
+            s, d = part.at[b, x, rest[way], cols(p)], zz[way].at[0, rest[way], cols(p)]
         elif kind == 3:
             s, d = zz[way].at[0, :, cols(p)], zz[way].at[1, :, cols(p)]
         else:
@@ -309,7 +294,7 @@
                 b, _ = target(way, k)
                 if k == 3:
                     copy_z(p, way, 0).wait_recv()
-                    z4[way][:, cols(p)] = z4[way][:, cols(p)] + acc[b, trav[way], cols(p)]
+                    z4[way][:, cols(p)] = z4[way][:, cols(p)] + part[b, x, trav[way], cols(p)]
                     copy_z(p, way, 1).start()
                 else:
                     got = 2 - k
@@ -318,12 +303,12 @@
                         copy_z(p, way, 2).wait_recv()
                     else:
                         copy_z(p, way, 3).wait_recv()
-                    zz[way][got, :, cols(p)] = zz[way][got, :, cols(p)] + acc[b, :, cols(p)]
+                    zz[way][got, :, cols(p)] = zz[way][got, :, cols(p)] + part[b, x, :, cols(p)]
                     copy_z(p, way, 5 - k).start()
 
     def copy_c(p):
         return remote(
-            acc.at[zl, pl.ds((1 - c) * 32, 32), cols(p)], fin.at[:, cols(p)], s_c.at[p], r_c.at[p], d_mate
+            part.at[zl, x, pl.ds((1 - c) * 32, 32), cols(p)], fin.at[:, cols(p)], s_c.at[p], r_c.at[p], d_mate
         )
 
     def z_final(p):
@@ -331,9 +316,9 @@
         def _():
             copy_z(p, 0, 4).wait_recv()
             copy_z(p, 1, 4).wait_recv()
-            acc[zl, :, cols(p)] = acc[zl, :, cols(p)] + (zp[2, :, cols(p)] + zm[2, :, cols(p)])
+            part[zl, x, :, cols(p)] = part[zl, x, :, cols(p)] + (zp[2, :, cols(p)] + zm[2, :, cols(p)])
             copy_c(p).start()
-            fin[:, cols(p)] = acc[zl, pl.ds(c * 32, 32), cols(p)]
+            fin[:, cols(p)] = part[zl, x, pl.ds(c * 32, 32), cols(p)]
 
     olds = (old_a, old_g)
     block = zl * 2 + lax.div(x, 2)
@@ -349,11 +334,10 @@
             ext[:, FEAT:EXT] = olds[p][0, :, 0:EXT - FEAT]
             old = ext[:, pl.ds(pl.multiple_of(block * 128, 128), WIN)]
             begin = SUM_COLS[p][0]
-            shard[:, at[0]:at[0] + WIN] = 0.5 * old + 0.5 * (fin[:, begin:begin + WIN] / total)
+            full[zl, x, c, :, at[0]:at[0] + WIN] = 0.5 * old + 0.5 * (fin[:, begin:begin + WIN] / total)
         else:
             begin = SUM_COLS[p][0]
-            shard[:, at[0]:at[0] + FEAT] = fin[:, begin:begin + FEAT] / total
-        full[zl, x, c, :, at[0]:at[0] + at[1]] = shard[:, at[0]:at[0] + at[1]]
+            full[zl, x, c, :, at[0]:at[0] + FEAT] = fin[:, begin:begin + FEAT] / total
 
     def acols(p):
         return pl.ds(ALL_COLS[p][0], ALL_COLS[p][1])
@@ -362,8 +346,7 @@
         origin = zl - (step - 1) if way == 0 else zl + (step - 1)
         ok = jnp.logical_and(origin >= 0, zl < 3) if way == 0 else jnp.logical_and(origin <= 3, zl > 0)
         ref = full.at[jnp.clip(origin, 0, 3), x, c, :, acols(p)]
-        s = shard.at[:, acols(p)] if step == 1 else ref
-        return ok, remote(s, ref, s_gz.at[p, way, step - 1], r_gz.at[p, way, step - 1], z_sides[way])
+        return ok, remote(ref, ref, s_gz.at[p, way, step - 1], r_gz.at[p, way, step - 1], z_sides[way])
 
     def gz_send(p, step):
         for way in range(2):
@@ -413,63 +396,91 @@
         for i in range(4):
             copy_gc(p, i).wait_recv()
 
+    for cp in locals_:
+        cp.wait()
+    first_rows(0)
+    send_rows(1)
+    second_rows(0)
+    last_rows(0)
+    for cp in quick:
+        cp.wait_recv()
+    held = jnp.zeros((8, ROWS), F32)
+    for s in range(8):
+        row = posb[s, pl.ds(lane, 1), :]
+        held = held + jnp.where(row >= 0, F32(1.0), F32(0.0))
+    count = jnp.sum(held[0:1, :])
+    part[:, :, :, 640:768] = jnp.full((4, 4, 64, 128), count, F32)
+    mate_rows(0)
+    pack(0)
+    factor_gram(0, 0, 2)
+    first_rows(1)
+    factor_gram(0, 2, 4)
     x_send(0, 0)
     x_send(0, 1)
+    second_rows(1)
+    x_relay(0)
+    last_rows(1)
+    mate_rows(1)
+    pack(1)
+    factor_gram(1, 0, 4)
     x_send(1, 0)
-    x_relay(0)
     x_send(1, 1)
-    x_send(2, 0)
-    x_relay(1)
     x_final(0)
     z_first(0)
+    cross_gram(0, 2)
+    z_step(0, 3)
+    cross_gram(2, 4)
+    z_step(0, 2)
+    x_relay(1)
+    x_send(2, 0)
     x_send(2, 1)
-    x_relay(2)
-    z_step(0, 3)
+    z_step(0, 1)
+    z_final(0)
     x_final(1)
     z_first(1)
-    z_step(0, 2)
+    make_shard(0)
+    gz_send(0, 1)
     z_step(1, 3)
-    z_step(0, 1)
+    gz_wait(0, 1)
+    gz_send(0, 2)
+    z_step(1, 2)
+    gz_wait(0, 2)
+    gz_send(0, 3)
+    x_relay(2)
+    z_step(1, 1)
+    z_final(1)
+    make_shard(1)
+    gz_send(1, 1)
+    gz_wait(0, 3)
+    gx_send(0)
+    gz_wait(1, 1)
+    gz_send(1, 2)
+    gz_wait(1, 2)
+    gz_send(1, 3)
+    gz_wait(1, 3)
+    gx_send(1)
     x_final(2)
     z_first(2)
-    z_step(1, 2)
-    z_final(0)
+    gx_forward(0)
     z_step(2, 3)
-    z_step(1, 1)
-    make_shard(0)
-    gz_send(0, 1)
     z_step(2, 2)
-    z_final(1)
+    gx_forward(1)
     z_step(2, 1)
-    gz_wait(0, 1)
-    gz_send(0, 2)
-    make_shard(1)
-    gz_send(1, 1)
     z_final(2)
-    gz_wait(0, 2)
-    gz_send(0, 3)
     make_shard(2)
     gz_send(2, 1)
-    gz_wait(1, 1)
-    gz_send(1, 2)
-    gz_wait(0, 3)
-    gx_send(0)
+    gx_last(0)
     gz_wait(2, 1)
     gz_send(2, 2)
-    gz_wait(1, 2)
-    gz_send(1, 3)
+    gx_last(1)
     gz_wait(2, 2)
     gz_send(2, 3)
-    gz_wait(1, 3)
-    gx_forward(0)
-    gx_send(1)
+    for cp in started:
+        cp.wait_send()
     gz_wait(2, 3)
-    gx_last(0)
-    gx_forward(1)
     gx_send(2)
-    gx_last(1)
-    gx_forward(2)
-
+
+    fac = raw_a
     row_ids = lax.broadcasted_iota(jnp.int32, (128, FEAT), 0)
     col_ids = lax.broadcasted_iota(jnp.int32, (128, FEAT), 1)
     alphas, damps = [], []
@@ -483,7 +494,6 @@
             return got.reshape(128, 128)
 
         def build(i, tr, t=t, first=first):
-            at = pl.ds(pl.multiple_of(i * 128, 128), 128)
             for k in range(8):
                 j = lax.rem(i + k, 8)
                 if k <= 4:
@@ -492,46 +502,55 @@
                     blk = rows_of(j, pl.ds(first + (8 - k) * 128, 128)).T
                 if k == 0:
                     tr = tr + jnp.sum(jnp.where(row_ids[:, :128] == col_ids[:, :128], blk, F32(0.0)))
-                fac[t, at, pl.ds(pl.multiple_of(j * 128, 128), 128)] = blk
+                fac[pl.ds(pl.multiple_of(t * FEAT + i * 128, 128), 128), pl.ds(pl.multiple_of(j * 128, 128), 128)] = blk
             return tr
 
         trace = lax.fori_loop(0, 8, build, F32(0.0))
         damp = F32(0.1) * trace / F32(FEAT)
 
-        def shift(i, best, t=t, damp=damp):
-            at = pl.ds(pl.multiple_of(i * 128, 128), 128)
-            m = fac[t, at, :] + jnp.where(row_ids + i * 128 == col_ids, damp, F32(0.0))
+        def shift(i, best, t=t, damp=damp, row=0, col=t * FEAT, skip=0):
+            at = pl.ds(pl.multiple_of(row + (i - skip) * 128, 128), 128)
+            m = fac[pl.ds(pl.multiple_of(t * FEAT + i * 128, 128), 128), :] + jnp.where(
+                row_ids + i * 128 == col_ids, damp, F32(0.0))
             hi, lo = split(m)
-            mh[t, at, :] = hi
-            ml[t, at, :] = lo
+            pkh[at, col:col + FEAT] = hi
+            pkl[at, col:col + FEAT] = lo
             return jnp.maximum(best, jnp.max(jnp.sum(jnp.abs(m), axis=1, keepdims=True)))
 
-        best = lax.fori_loop(0, 8, shift, F32(0.0))
+        best = lax.fori_loop(0, 6, shift, F32(0.0))
+        best = lax.fori_loop(
+            6, 8, lambda i, best, t=t: shift(i, best, row=t * 256, col=2 * FEAT, skip=6), best)
         alphas.append(F32(1.0) / jnp.full((1, 1), best, F32))
         damps.append(damp)
         if t == 0:
+            gx_forward(2)
+        else:
             gx_last(2)
 
     d = zl * 8 + x * 2 + c
     mine = pl.ds(pl.multiple_of(d * 32, 32), 32)
-    out_a[0] = fac[0, mine, :]
-    out_g[0] = fac[1, mine, :]
+    mine_g = pl.ds(pl.multiple_of(FEAT + d * 32, 32), 32)
+    out[0] = fac[mine, :]
+    out[1] = fac[mine_g, :]
 
     def times(v, t):
         hi, lo = split(v)
         both = jnp.concatenate([hi, lo], axis=0)
         parts = []
         for nb in range(4):
-            at = slice(nb * 256, nb * 256 + 256)
-            one = dot(both, mh[t, :, at])
-            parts.append(one[:32] + (one[32:] + dot(hi, ml[t, :, at])))
+            at = slice(t * FEAT + nb * 256, t * FEAT + nb * 256 + 256)
+            low = slice(2 * FEAT + nb * 256, 2 * FEAT + nb * 256 + 256)
+            end = slice(t * 256, t * 256 + 256)
+            one = dot(both[:, :SLOTS], pkh[:, at]) + dot(both[:, SLOTS:], pkh[end, low])
+            fine = dot(hi[:, :SLOTS], pkl[:, at]) + dot(hi[:, SLOTS:], pkl[end, low])
+            parts.append(one[:32] + (one[32:] + fine))
         return jnp.concatenate(parts, axis=1)
 
     aa, ag = alphas
     unit_rows = jnp.where(
         lax.broadcasted_iota(jnp.int32, (32, FEAT), 0) + d * 32
         == lax.broadcasted_iota(jnp.int32, (32, FEAT), 1), F32(1.0), F32(0.0))
-    shifted_rows = fac[1, mine, :] + damps[1] * unit_rows
+    shifted_rows = fac[mine_g, :] + damps[1] * unit_rows
     u1 = ag * (2.0 * unit_rows - ag * shifted_rows)
     u2 = times(u1, 1)
     inv_rows = 2.0 * u1 - ag * (2.0 * u2 - ag * times(u2, 1))
@@ -546,10 +565,7 @@
     lhs = jnp.concatenate(parts, axis=1)
     half_way = aa * (2.0 * lhs - aa * times(lhs, 0))
     w = times(half_way, 0)
-    precond = 2.0 * half_way - aa * (2.0 * w - aa * times(w, 0))
-    moment = 0.9 * mom[0] + precond
-    out_m[0] = moment
-    out_w[0] = wts[0] - 0.5 * moment
+    out[2] = 2.0 * half_way - aa * (2.0 * w - aa * times(w, 0))
 
     for p in range(3):
         for way in range(2):
@@ -574,6 +590,14 @@
             copy_gc(p, i).wait_send()
 
 
+def finish_kernel(got, mom, wts, out_a, out_g, out_m, out_w):
+    out_a[0] = got[0]
+    out_g[0] = got[1]
+    moment = 0.9 * mom[0] + got[2]
+    out_m[0] = moment
+    out_w[0] = wts[0] - 0.5 * moment
+
+
 def on_device(acts, grads_out, routes, counts, old_act_factor, old_grad_factor, momentum, weights):
     experts = jnp.arange(8, dtype=jnp.int32)
     hit = jnp.sum(
@@ -585,55 +609,46 @@
     vm = pl.BlockSpec(memory_space=pltpu.VMEM)
     hbm = pl.BlockSpec(memory_space=pl.ANY)
     dma = pltpu.SemaphoreType.DMA
-    sums = pl.pallas_call(
-        gather_kernel,
-        out_shape=jax.ShapeDtypeStruct((FEAT, SUM_W), F32),
-        in_specs=[hbm, hbm, hbm],
+    got = pl.pallas_call(
+        step_kernel,
+        out_shape=jax.ShapeDtypeStruct((3, 32, FEAT), F32),
+        in_specs=[hbm, hbm, hbm, vm, vm],
         out_specs=vm,
         scratch_shapes=[
             pltpu.VMEM((8 * ROWS, FEAT), F32),
             pltpu.VMEM((8 * ROWS, FEAT), F32),
             pltpu.VMEM((8, 8, ROWS), jnp.int32),
-            pltpu.VMEM((8 * CAP, 2 * EXT), BF16),
-            pltpu.VMEM((8 * CAP, 2 * EXT), BF16),
-            dma((3,)), dma((2, 2, 2)), dma((2, 2, 2)), dma((2, 2)), dma((2, 2)),
-            dma((4, 2, 2)), dma((4, 2, 2)), dma((8,)), dma((8,)),
-        ],
-        compiler_params=pltpu.CompilerParams(
-            collective_id=0, has_side_effects=True, vmem_limit_bytes=60 * 1024 * 1024
-        ),
-        name="gather_rows",
-    )(acts, grads_out, pos)
-    out = jax.ShapeDtypeStruct((1, 32, FEAT), F32)
-    return pl.pallas_call(
-        reduce_kernel,
-        out_shape=(out, out, out, out),
-        in_specs=[vm] * 5,
-        out_specs=[vm] * 4,
-        scratch_shapes=[
+            pltpu.VMEM((SLOTS, 2 * EXT), BF16),
+            pltpu.VMEM((SLOTS, 2 * EXT), BF16),
+            pltpu.VMEM((4, 4, 64, SUM_W), F32),
             pltpu.VMEM((2, 4, 32, SUM_W), F32),
             pltpu.VMEM((2, 4, 32, SUM_W), F32),
             pltpu.VMEM((2, 4, 32, SUM_W), F32),
-            pltpu.VMEM((4, 64, SUM_W), F32),
             pltpu.VMEM((32, SUM_W), F32),
             pltpu.VMEM((32, SUM_W), F32),
             pltpu.VMEM((3, 64, SUM_W), F32),
             pltpu.VMEM((3, 64, SUM_W), F32),
             pltpu.VMEM((32, SUM_W), F32),
-            pltpu.VMEM((32, ALL_W), F32),
             pltpu.VMEM((4, 4, 2, 32, ALL_W), F32),
             pltpu.VMEM((32, EXT), F32),
-            pltpu.VMEM((2, FEAT, FEAT), F32),
-            pltpu.VMEM((2, FEAT, FEAT), BF16),
-            pltpu.VMEM((2, FEAT, FEAT), BF16),
+            dma((3,)), dma((2, 2, 2)), dma((2, 2, 2)), dma((2, 2)), dma((2, 2)),
+            dma((4, 2, 2)), dma((4, 2, 2)), dma((8,)), dma((8,)),
             dma((3, 2, 3)), dma((3, 2, 3)), dma((3, 2, 5)), dma((3, 2, 5)), dma((3,)), dma((3,)),
             dma((3, 2, 3)), dma((3, 2, 3)), dma((3, 2, 2)), dma((3, 2, 2)), dma((3, 4)), dma((3, 4)),
         ],
         compiler_params=pltpu.CompilerParams(
-            collective_id=1, has_side_effects=True, vmem_limit_bytes=63 * 1024 * 1024
+            collective_id=0, has_side_effects=True, vmem_limit_bytes=67043328
         ),
-        name="reduce_apply",
-    )(sums.reshape(4, 4, 64, SUM_W), old_act_factor, old_grad_factor, momentum, weights)
+        name="step",
+    )(acts, grads_out, pos, old_act_factor, old_grad_factor)
+    out = jax.ShapeDtypeStruct((1, 32, FEAT), F32)
+    return pl.pallas_call(
+        finish_kernel,
+        out_shape=(out, out, out, out),
+        in_specs=[vm] * 3,
+        out_specs=[vm] * 4,
+        name="finish",
+    )(got, momentum, weights)
 
 
 def solution(mesh):

time: 289 us -> 217 us (0.75)
  Pallas kernels: 278 us -> 213 us
  local copies, waits for them, and re-layouts: 6.49 us -> 1.55 us
    pallas_call x2, Pallas kernels: 278 us -> 213 us  [the longest x1 211 us: on_device(): pl.pallas_call(step_kernel, out_shape=jax.ShapeDtypeStruct((3, 32, FEAT),...]
    unnamed x4, local copies, waits for them, and re-layouts: 6.27 us -> 1.33 us
where the time goes in v2:
time: 217 us
  Pallas kernels  213 us (98%)
    pallas_call x1, Pallas kernels, on_device(): pl.pallas_call(step_kernel, out_shape=jax.ShapeDtypeStruct((3, 32, FEAT),...  211 us

profile of v2, /device:TPU:1, one launch (start us, length us, event | category | flops | bytes accessed | tf_op | source)
XLA Modules:
  0.0 216.7 jit_solution(5325569455201755312)
XLA Ops:
  0.6 0.0 copy-start
  0.6 0.7 copy-done
  1.3 0.6 reduce-window.6
  1.9 0.2 slice_reduce_fusion
  2.1 0.0 copy-start.1
  2.1 0.7 copy-done.1
  2.8 0.7 and_select_fusion.pos
  3.5 211.4 %step.1.got = f32[3,32,1024]{2,1,0:T(8,128)} custom-call(f32[256,1024]{1,0:T(8,128)} %acts.1, f32[256,1024]{1,0:T(8,128)} %grads.1, s32[8,256]{1,0:T(8,128)} %and_select_fusion.pos, f32[1,32,1024]{2,1,0:T(8,128)} %old_a.1, f32[1,32,1024]{2,1,0:T(8,128)} %old_g.1), custom_call_target="tpu_custom_call" | custom-call | tf_op jit(solution)/shard_map/step/pallas_call | solution.py:612
  214.8 1.9 finish.1
  (3 shorter events, 0.0 us)
Async XLA Ops:
  0.6 0.7 copy-start
  2.1 0.7 copy-start.1

commit v3 on v2

--- a/solution.py
+++ b/solution.py
@@ -14,8 +14,8 @@
 SLOTS = 8 * CAP
 WIN = 640
 EXT = 1536
-SUM_COLS = ((0, 768), (768, 640), (1408, 1024))
-SUM_W = 2432
+SUM_COLS = ((0, 640), (640, 640), (1280, 1024))
+SUM_W = 2304
 ALL_COLS = ((0, 640), (640, 640), (1280, 1024))
 ALL_W = 2304
 
@@ -55,7 +55,7 @@
 
 
 def step_kernel(
-    acts, grads, pos, old_a, old_g, out,
+    acts, grads, routes, counts, old_a, old_g, out,
     raw_a, raw_g, posb, pkh, pkl, part,
     x1, x2a, x2b, z4p, z4m, zp, zm, fin, full, ext,
     loc, s_y, r_y, s_f, r_f, s_p, r_p, s_q, r_q,
@@ -95,7 +95,6 @@
     locals_ = [
         pltpu.make_async_copy(src[t], raw[t].at[pl.ds(0, ROWS), :], loc.at[t]) for t in range(2)
     ]
-    locals_.append(pltpu.make_async_copy(pos, posb.at[0], loc.at[2]))
     for cp in locals_:
         cp.start()
     toward = (d_up, d_down)
@@ -117,9 +116,20 @@
             go(mate[0, t, half])
 
     send_rows(0)
+    expert_ids = lax.broadcasted_iota(jnp.int32, (8, ROWS), 0)
+    hit = jnp.where(routes[0:1, :] == expert_ids, F32(1.0), F32(0.0)) + jnp.where(
+        routes[1:2, :] == expert_ids, F32(1.0), F32(0.0))
+    before = jnp.where(
+        lax.broadcasted_iota(jnp.int32, (ROWS, ROWS), 0) < lax.broadcasted_iota(jnp.int32, (ROWS, ROWS), 1),
+        F32(1.0), F32(0.0)).astype(BF16)
+    rank = dot(hit.astype(BF16), before)
+    square = lax.broadcasted_iota(jnp.int32, (8, 8), 0) == lax.broadcasted_iota(jnp.int32, (8, 8), 1)
+    limit = jnp.sum(
+        jnp.where(square, jnp.broadcast_to(counts[...].astype(F32), (8, 8)), F32(0.0)), axis=1, keepdims=True)
+    posb[0] = jnp.where(jnp.logical_and(hit > 0.0, rank < limit), rank, F32(-1.0))
     quick = []
     for i, peer in enumerate(peers):
-        quick.append(remote(pos, posb.at[i + 1], s_q.at[i + 1], r_q.at[i + 1], peer))
+        quick.append(remote(posb.at[0], posb.at[i + 1], s_q.at[i + 1], r_q.at[i + 1], peer))
         go(quick[-1])
 
     def relay(slot, t, half):
@@ -130,7 +140,7 @@
         go(mate[slot, t, half])
 
     lane = c * 4 + y
-    slot_ids = lax.broadcasted_iota(jnp.int32, (CAP, ROWS), 0)
+    slot_ids = lax.broadcasted_iota(jnp.int32, (CAP, ROWS), 0).astype(F32)
 
     def pack(t):
         def body(s, carry):
@@ -175,7 +185,7 @@
         return store
 
     def cross_store(ib, nb, got):
-        part[ib, :, :, 1408 + nb * 256:1408 + nb * 256 + 256] = got.reshape(4, 64, 256)
+        part[ib, :, :, 1280 + nb * 256:1280 + nb * 256 + 256] = got.reshape(4, 64, 256)
 
     def factor_gram(t, begin_block, end_block):
         gram(t * EXT, lambda at: t * EXT + at, 768, window_store(SUM_COLS[t][0]), begin_block, end_block)
@@ -327,7 +337,7 @@
         @pl.when(jnp.logical_not(home))
         def _():
             copy_c(p).wait_recv()
-        total = jnp.maximum(fin[0:1, 640:641], F32(1.0))
+        total = jnp.maximum(fin[8:9, 512:513], F32(1.0))
         at = ALL_COLS[p]
         if p < 2:
             ext[:, 0:FEAT] = olds[p][0]
@@ -409,12 +419,19 @@
         row = posb[s, pl.ds(lane, 1), :]
         held = held + jnp.where(row >= 0, F32(1.0), F32(0.0))
     count = jnp.sum(held[0:1, :])
-    part[:, :, :, 640:768] = jnp.full((4, 4, 64, 128), count, F32)
     mate_rows(0)
     pack(0)
     factor_gram(0, 0, 2)
     first_rows(1)
     factor_gram(0, 2, 4)
+    lanes = lax.broadcasted_iota(jnp.int32, (64, 128), 1)
+    tops = lax.broadcasted_iota(jnp.int32, (64, 128), 0)
+    for b in range(4):
+        for xb in range(4):
+            put = lanes == 0
+            if b >= 2 and xb % 2 == 0:
+                put = jnp.logical_and(put, tops > 0)
+            part[b, xb, :, 512:640] = jnp.where(put, count, part[b, xb, :, 512:640])
     x_send(0, 0)
     x_send(0, 1)
     second_rows(1)
@@ -496,7 +513,15 @@
         def build(i, tr, t=t, first=first):
             for k in range(8):
                 j = lax.rem(i + k, 8)
-                if k <= 4:
+                if k == 4 and t == 0:
+                    i_low = lax.rem(i, 4)
+                    one = rows_of(i_low, pl.ds(first + 512, 128))
+                    two = rows_of(i_low + 4, pl.ds(first + 512, 128))
+                    blk = jnp.where(
+                        i < 4,
+                        jnp.where(col_ids[:, :128] == 0, two.T, one),
+                        jnp.where(row_ids[:, :128] == 0, two, one.T))
+                elif k <= 4:
                     blk = rows_of(i, pl.ds(first + k * 128, 128))
                 else:
                     blk = rows_of(j, pl.ds(first + (8 - k) * 128, 128)).T
@@ -599,25 +624,18 @@
 
 
 def on_device(acts, grads_out, routes, counts, old_act_factor, old_grad_factor, momentum, weights):
-    experts = jnp.arange(8, dtype=jnp.int32)
-    hit = jnp.sum(
-        (routes.T[:, None, :] == experts[None, :, None]).astype(jnp.int32), axis=0, dtype=jnp.int32
-    )
-    rank = jnp.cumsum(hit, axis=1, dtype=jnp.int32) - hit
-    kept = (hit > 0) & (rank < counts[0][:, None])
-    pos = jnp.where(kept, rank, -1)
     vm = pl.BlockSpec(memory_space=pltpu.VMEM)
     hbm = pl.BlockSpec(memory_space=pl.ANY)
     dma = pltpu.SemaphoreType.DMA
     got = pl.pallas_call(
         step_kernel,
         out_shape=jax.ShapeDtypeStruct((3, 32, FEAT), F32),
-        in_specs=[hbm, hbm, hbm, vm, vm],
+        in_specs=[hbm, hbm, vm, vm, vm, vm],
         out_specs=vm,
         scratch_shapes=[
             pltpu.VMEM((8 * ROWS, FEAT), F32),
             pltpu.VMEM((8 * ROWS, FEAT), F32),
-            pltpu.VMEM((8, 8, ROWS), jnp.int32),
+            pltpu.VMEM((8, 8, ROWS), F32),
             pltpu.VMEM((SLOTS, 2 * EXT), BF16),
             pltpu.VMEM((SLOTS, 2 * EXT), BF16),
             pltpu.VMEM((4, 4, 64, SUM_W), F32),
@@ -631,7 +649,7 @@
             pltpu.VMEM((32, SUM_W), F32),
             pltpu.VMEM((4, 4, 2, 32, ALL_W), F32),
             pltpu.VMEM((32, EXT), F32),
-            dma((3,)), dma((2, 2, 2)), dma((2, 2, 2)), dma((2, 2)), dma((2, 2)),
+            dma((2,)), dma((2, 2, 2)), dma((2, 2, 2)), dma((2, 2)), dma((2, 2)),
             dma((4, 2, 2)), dma((4, 2, 2)), dma((8,)), dma((8,)),
             dma((3, 2, 3)), dma((3, 2, 3)), dma((3, 2, 5)), dma((3, 2, 5)), dma((3,)), dma((3,)),
             dma((3, 2, 3)), dma((3, 2, 3)), dma((3, 2, 2)), dma((3, 2, 2)), dma((3, 4)), dma((3, 4)),
@@ -640,7 +658,7 @@
             collective_id=0, has_side_effects=True, vmem_limit_bytes=67043328
         ),
         name="step",
-    )(acts, grads_out, pos, old_act_factor, old_grad_factor)
+    )(acts, grads_out, routes.T, counts, old_act_factor, old_grad_factor)
     out = jax.ShapeDtypeStruct((1, 32, FEAT), F32)
     return pl.pallas_call(
         finish_kernel,

time: 217 us -> 214 us (0.986)
  no operation moved by 1% of the time
where the time goes in v3:
time: 214 us
  Pallas kernels  213 us (100%)
    pallas_call x1, Pallas kernels, on_device(): pl.pallas_call(step_kernel, out_shape=jax.ShapeDtypeStruct((3, 32, FEAT),...  212 us

profile of v3, /device:TPU:1, one launch (start us, length us, event | category | flops | bytes accessed | tf_op | source)
XLA Modules:
  0.0 214.1 jit_solution(14380427970822710707)
XLA Ops:
  0.6 211.6 %step.1.got = f32[3,32,1024]{2,1,0:T(8,128)} custom-call(f32[256,1024]{1,0:T(8,128)} %acts.1, f32[256,1024]{1,0:T(8,128)} %grads.1, s32[2,256]{1,0:T(2,128)} %bitcast.1, s32[1,8]{1,0:T(1,128)} %counts.1, f32[1,32,1024]{2,1,0:T(8,128)} %old_a.1, f32[1,32,1024]{2,1,0:T(8,128)} %old_g.1), custom_call_target="tpu_custom_call" | custom-call | tf_op jit(solution)/shard_map/step/pallas_call | solution.py:630
  212.2 1.9 finish.1

commit v4 on v3

--- a/solution.py
+++ b/solution.py
@@ -460,10 +460,10 @@
     z_step(1, 3)
     gz_wait(0, 1)
     gz_send(0, 2)
+    x_relay(2)
     z_step(1, 2)
     gz_wait(0, 2)
     gz_send(0, 3)
-    x_relay(2)
     z_step(1, 1)
     z_final(1)
     make_shard(1)

time: 214 us -> 214 us (level)
  no operation moved by 1% of the time
where the time goes in v4:
time: 214 us
  Pallas kernels  213 us (100%)
    pallas_call x1, Pallas kernels, on_device(): pl.pallas_call(step_kernel, out_shape=jax.ShapeDtypeStruct((3, 32, FEAT),...  212 us

profile of v4, /device:TPU:1, one launch (start us, length us, event | category | flops | bytes accessed | tf_op | source)
XLA Modules:
  0.0 214.1 jit_solution(2232727931120118407)
XLA Ops:
  0.6 211.6 %step.1.got = f32[3,32,1024]{2,1,0:T(8,128)} custom-call(f32[256,1024]{1,0:T(8,128)} %acts.1, f32[256,1024]{1,0:T(8,128)} %grads.1, s32[2,256]{1,0:T(2,128)} %bitcast.1, s32[1,8]{1,0:T(1,128)} %counts.1, f32[1,32,1024]{2,1,0:T(8,128)} %old_a.1, f32[1,32,1024]{2,1,0:T(8,128)} %old_g.1), custom_call_target="tpu_custom_call" | custom-call | tf_op jit(solution)/shard_map/step/pallas_call | solution.py:630
  212.2 1.9 finish.1
